TPU v7x, 128 devices: a whole 4x4x4 slice. The times are simulated.
128 devices in a mesh: pr: 16 (over z, x), pc: 8 (over y, core).
Axes of the slice: x: 4, y: 4, z: 4, core: 2. Of those that a mesh axis runs over, the one named last changes fastest.
Arguments:
- trailing: float32 [20480, 20480], P('pr', 'pc'), may hold values from -25 to 25, as said below
- v_panels: float32 [6, 32, 20480], P(None, None, ('pr', 'pc')), may hold values from -0.078125 to 0.078125
- t_panels: float32 [6, 32, 32], replicated, may hold values from -0.2 to 0.5, as said below
Outputs:
- updated: float32 [20480, 20480], P('pr', 'pc')
- w_panels: float32 [6, 32, 20480], P(None, None, ('pr', 'pc'))
Inputs may be any that keep to these rules, and one draw needn't show every extreme that they name: trailing is exactly symmetric. `t_panels`: each panel's factor is upper triangular with diagonal entries of 0.25 to 0.5.
All inputs are finite; a program needn't handle non-finite values.
Results may differ from a plain program's by a relative error of at most 0.00013.
Values sent between devices are 32-bit elements; how exact they have to be, the bound alone decides.
A program may use at most 128 MiB of HBM per device.

v0:
```python
import jax
import jax.numpy as jnp
from jax import lax
from jax.sharding import PartitionSpec as P


def broadcast(value, axis, source):
    kept = jnp.where(lax.axis_index(axis) == source, value, 0).astype(value.dtype)
    return lax.psum(kept, axis)


def contract(left_side, right_side, left_dim, right_dim):
    return lax.dot_general(
        left_side,
        right_side,
        (((left_dim,), (right_dim,)), ((), ())),
        precision=lax.Precision.HIGHEST,
        preferred_element_type=jnp.float32,
    )


def fetch_v_columns(v_row, col_rank, ratio):
    pieces = []
    for offset in range(ratio):
        pieces.append(broadcast(v_row, "pr", col_rank * ratio + offset))
    return jnp.concatenate(pieces, axis=1)


def fetch_w_columns(w_row, col_rank, ratio):
    pieces = []
    for offset in range(ratio):
        pieces.append(broadcast(w_row, "pr", col_rank * ratio + offset))
    return jnp.concatenate(pieces, axis=1)


def per_device(trailing, v_panels, t_panels):
    matrix = trailing
    rows_here = matrix.shape[0]
    col_rank = lax.axis_index("pc")
    ratio = lax.axis_size("pr") // lax.axis_size("pc")
    share = rows_here // lax.axis_size("pc")
    w_blocks = []
    for panel in range(v_panels.shape[0]):
        v_row = lax.all_gather(v_panels[panel], "pc", axis=1, tiled=True)
        v_col = fetch_v_columns(v_row, col_rank, ratio)
        factor = t_panels[panel]
        partial_value = contract(v_col, matrix, 1, 1)
        x_row = lax.psum(partial_value, "pc")
        gram_block = lax.psum(contract(v_row, x_row, 1, 1), "pr")
        middle = contract(contract(factor, gram_block, 0, 0), factor, 1, 0)
        w_row = contract(factor, x_row, 0, 0) - 0.5 * contract(middle, v_row, 0, 0)
        w_col = fetch_w_columns(w_row, col_rank, ratio)
        left_side = jnp.concatenate([v_row, w_row], axis=0)
        right_side = jnp.concatenate([w_col, v_col], axis=0)
        matrix = matrix - contract(left_side, right_side, 0, 0)
        w_blocks.append(lax.dynamic_slice_in_dim(w_row, col_rank * share, share, 1))
    return (matrix, jnp.stack(w_blocks))


def solution(mesh):
    return jax.shard_map(
        per_device,
        mesh=mesh,
        in_specs=(P("pr", "pc"), P(None, None, ("pr", "pc")), P()),
        out_specs=(P("pr", "pc"), P(None, None, ("pr", "pc"))),
        check_vma=False,
    )
```

profile of v0, /device:TPU:0, one launch (start us, length us, event | category | flops | bytes accessed | tf_op | source)
XLA Modules:
  0.0 1610.5 jit_solution(2257900202977496059)
XLA Ops:
  8.2 13.8 all-gather
  23.3 13.2 all-gather.1
  36.9 71.9 %all-reduce.45.cloned.1.call-done = (f32[32,1280]{1,0:T(8,128)}, f32[32,1280]{1,0:T(8,128)}) async-done(((f32[32,1280]{1,0:T(8,128)}, f32[32,1280]{1,0:T(8,128)}), (f32[32,1280]{1,0:T(8,128)}, f32[32,1280]{1,0:T(8,128)})) %all-reduce.45.cloned.1.call-update) | async-done | bytes 327696 | tf_op jit(solution)/shard_map/psum | solution.py:9
  110.6 15.3 fusion.109
  126.8 56.5 %all-reduce.21.cloned.1.call-done = f32[32,1280]{1,0:T(8,128)} async-done(((f32[32,1280]{1,0:T(8,128)}), f32[32,1280]{1,0:T(8,128)}) %all-reduce.21.cloned.1.call-update) | async-done | bytes 163856 | tf_op jit(solution)/shard_map/psum | solution.py:48
  184.6 74.6 %psum.255 = f32[32,32]{0,1:T(8,128)S(1)} all-reduce(f32[32,32]{0,1:T(8,128)S(1)} %convolution_bitcast_fusion.11), channel_id=1, replica_groups=mesh['pr'=16,'pc'=8] {'pr'}, use_global_device_ids=true, to_apply=%region_3.4 | all-reduce | flops 1024 | bytes 8192 | tf_op jit(solution)/shard_map/psum | solution.py:49
  262.5 13.5 all-gather.2
  276.3 65.5 %all-reduce.43.cloned.1.call-done = (f32[32,1280]{1,0:T(8,128)}, f32[32,1280]{1,0:T(8,128)}, f32[32,1280]{1,0:T(8,128)}, f32[32,1280]{1,0:T(8,128)}) async-done(((f32[32,1280]{1,0:T(8,128)}, f32[32,1280]{1,0:T(8,128)}, f32[32,1280]{1,0:T(8,128)}, f32[32,1280]{1,0:T(8,128)}), (f32[32,1280]{1,0:T(8,128)}, f32[32,1280]{1,0:T(8,128)}, f32[32,1280]{1,0:T(8,128)}, ...) | async-done | bytes 655376 | tf_op jit(solution)/shard_map/psum | solution.py:9
  343.7 14.6 convolution_subtract_fusion.5
  376.5 56.5 %all-reduce.23.cloned.1.call-done = f32[32,1280]{1,0:T(8,128)} async-done(((f32[32,1280]{1,0:T(8,128)}), f32[32,1280]{1,0:T(8,128)}) %all-reduce.23.cloned.1.call-update) | async-done | bytes 163856 | tf_op jit(solution)/shard_map/psum | solution.py:48
  434.4 74.6 %psum.261 = f32[32,32]{0,1:T(8,128)S(1)} all-reduce(f32[32,32]{0,1:T(8,128)S(1)} %convolution_bitcast_fusion.10), channel_id=1, replica_groups=mesh['pr'=16,'pc'=8] {'pr'}, use_global_device_ids=true, to_apply=%region_9.10 | all-reduce | flops 1024 | bytes 8192 | tf_op jit(solution)/shard_map/psum | solution.py:49
  512.2 13.2 all-gather.3
  537.6 54.1 %all-reduce.41.cloned.1.call-done = (f32[32,1280]{1,0:T(8,128)}, f32[32,1280]{1,0:T(8,128)}, f32[32,1280]{1,0:T(8,128)}, f32[32,1280]{1,0:T(8,128)}) async-done(((f32[32,1280]{1,0:T(8,128)}, f32[32,1280]{1,0:T(8,128)}, f32[32,1280]{1,0:T(8,128)}, f32[32,1280]{1,0:T(8,128)}), (f32[32,1280]{1,0:T(8,128)}, f32[32,1280]{1,0:T(8,128)}, f32[32,1280]{1,0:T(8,128)}, ...) | async-done | bytes 655376 | tf_op jit(solution)/shard_map/psum | solution.py:9
  593.5 14.2 convolution_subtract_fusion.4
  626.0 56.5 %all-reduce.25.cloned.1.call-done = f32[32,1280]{1,0:T(8,128)} async-done(((f32[32,1280]{1,0:T(8,128)}), f32[32,1280]{1,0:T(8,128)}) %all-reduce.25.cloned.1.call-update) | async-done | bytes 163856 | tf_op jit(solution)/shard_map/psum | solution.py:48
  683.9 74.6 %psum.267 = f32[32,32]{0,1:T(8,128)S(1)} all-reduce(f32[32,32]{0,1:T(8,128)S(1)} %convolution_bitcast_fusion.9), channel_id=1, replica_groups=mesh['pr'=16,'pc'=8] {'pr'}, use_global_device_ids=true, to_apply=%region_15.16 | all-reduce | flops 1024 | bytes 8192 | tf_op jit(solution)/shard_map/psum | solution.py:49
  761.8 13.2 all-gather.4
  775.7 65.4 %all-reduce.39.cloned.1.call-done = (f32[32,1280]{1,0:T(8,128)}, f32[32,1280]{1,0:T(8,128)}, f32[32,1280]{1,0:T(8,128)}, f32[32,1280]{1,0:T(8,128)}) async-done(((f32[32,1280]{1,0:T(8,128)}, f32[32,1280]{1,0:T(8,128)}, f32[32,1280]{1,0:T(8,128)}, f32[32,1280]{1,0:T(8,128)}), (f32[32,1280]{1,0:T(8,128)}, f32[32,1280]{1,0:T(8,128)}, f32[32,1280]{1,0:T(8,128)}, ...) | async-done | bytes 655376 | tf_op jit(solution)/shard_map/psum | solution.py:9
  843.0 14.2 convolution_subtract_fusion.3
  875.5 56.5 %all-reduce.27.cloned.1.call-done = f32[32,1280]{1,0:T(8,128)} async-done(((f32[32,1280]{1,0:T(8,128)}), f32[32,1280]{1,0:T(8,128)}) %all-reduce.27.cloned.1.call-update) | async-done | bytes 163856 | tf_op jit(solution)/shard_map/psum | solution.py:48
  933.4 74.6 %psum.273 = f32[32,32]{0,1:T(8,128)S(1)} all-reduce(f32[32,32]{0,1:T(8,128)S(1)} %convolution_bitcast_fusion.8), channel_id=1, replica_groups=mesh['pr'=16,'pc'=8] {'pr'}, use_global_device_ids=true, to_apply=%region_21.22 | all-reduce | flops 1024 | bytes 8192 | tf_op jit(solution)/shard_map/psum | solution.py:49
  1011.2 13.2 all-gather.5
  1025.0 65.7 %all-reduce.37.cloned.1.call-done = (f32[32,1280]{1,0:T(8,128)}, f32[32,1280]{1,0:T(8,128)}, f32[32,1280]{1,0:T(8,128)}, f32[32,1280]{1,0:T(8,128)}) async-done(((f32[32,1280]{1,0:T(8,128)}, f32[32,1280]{1,0:T(8,128)}, f32[32,1280]{1,0:T(8,128)}, f32[32,1280]{1,0:T(8,128)}), (f32[32,1280]{1,0:T(8,128)}, f32[32,1280]{1,0:T(8,128)}, f32[32,1280]{1,0:T(8,128)}, ...) | async-done | bytes 655376 | tf_op jit(solution)/shard_map/psum | solution.py:9
  1092.5 14.2 convolution_subtract_fusion.2
  1125.0 56.5 %all-reduce.29.cloned.1.call-done = f32[32,1280]{1,0:T(8,128)} async-done(((f32[32,1280]{1,0:T(8,128)}), f32[32,1280]{1,0:T(8,128)}) %all-reduce.29.cloned.1.call-update) | async-done | bytes 163856 | tf_op jit(solution)/shard_map/psum | solution.py:48
  1182.9 74.6 %psum.279 = f32[32,32]{0,1:T(8,128)S(1)} all-reduce(f32[32,32]{0,1:T(8,128)S(1)} %convolution_bitcast_fusion.7), channel_id=1, replica_groups=mesh['pr'=16,'pc'=8] {'pr'}, use_global_device_ids=true, to_apply=%region_27.28 | all-reduce | flops 1024 | bytes 8192 | tf_op jit(solution)/shard_map/psum | solution.py:49
  1260.8 79.3 %all-reduce.35.cloned.1.call-done = (f32[32,1280]{1,0:T(8,128)}, f32[32,1280]{1,0:T(8,128)}, f32[32,1280]{1,0:T(8,128)}, f32[32,1280]{1,0:T(8,128)}) async-done(((f32[32,1280]{1,0:T(8,128)}, f32[32,1280]{1,0:T(8,128)}, f32[32,1280]{1,0:T(8,128)}, f32[32,1280]{1,0:T(8,128)}), (f32[32,1280]{1,0:T(8,128)}, f32[32,1280]{1,0:T(8,128)}, f32[32,1280]{1,0:T(8,128)}, ...) | async-done | bytes 655376 | tf_op jit(solution)/shard_map/psum | solution.py:9
  1342.0 14.4 convolution_subtract_fusion.1
  1374.0 57.2 %all-reduce.31.cloned.1.call-done = f32[32,1280]{1,0:T(8,128)} async-done(((f32[32,1280]{1,0:T(8,128)}), f32[32,1280]{1,0:T(8,128)}) %all-reduce.31.cloned.1.call-update) | async-done | bytes 163856 | tf_op jit(solution)/shard_map/psum | solution.py:48
  1432.5 74.9 %psum.285 = f32[32,32]{0,1:T(8,128)S(1)} all-reduce(f32[32,32]{0,1:T(8,128)S(1)} %convolution_bitcast_fusion.6), channel_id=1, replica_groups=mesh['pr'=16,'pc'=8] {'pr'}, use_global_device_ids=true, to_apply=%region_33.34 | all-reduce | flops 1024 | bytes 8192 | tf_op jit(solution)/shard_map/psum | solution.py:49
  1510.9 77.3 %all-reduce.33.cloned.1.call-done = (f32[32,1280]{1,0:T(8,128)}, f32[32,1280]{1,0:T(8,128)}) async-done(((f32[32,1280]{1,0:T(8,128)}, f32[32,1280]{1,0:T(8,128)}), (f32[32,1280]{1,0:T(8,128)}, f32[32,1280]{1,0:T(8,128)})) %all-reduce.33.cloned.1.call-update) | async-done | bytes 327696 | tf_op jit(solution)/shard_map/psum | solution.py:9
  1588.1 15.4 convolution_subtract_fusion
  (112 shorter events, 146.5 us)
Async XLA Ops:
  7.2 252.0 %copy-start.5 = (f32[6,32,32]{2,1,0:T(8,128)S(1)}, f32[6,32,32]{2,1,0:T(8,128)}, u32[]{:S(2)}) copy-start(f32[6,32,32]{2,1,0:T(8,128)} %param.5) | copy-start | bytes 73732
  7.2 101.6 %all-reduce.45.cloned.1.call-start = ((), (), s32[]{:S(2)}) async-start(), calls=%async_computation.12 | async-start | bytes 655360 | tf_op jit(solution)/shard_map/psum | solution.py:9
  23.2 160.1 %all-reduce.21.cloned.1.call-start = ((), (), s32[]{:S(2)}) async-start(), calls=%async_computation | async-start | bytes 327680 | tf_op jit(solution)/shard_map/psum | solution.py:48
  126.0 215.9 %all-reduce.43.cloned.1.call-start = ((), (), s32[]{:S(2)}) async-start(), calls=%async_computation.11 | async-start | bytes 1310720 | tf_op jit(solution)/shard_map/psum | solution.py:9
  262.4 170.6 %all-reduce.23.cloned.1.call-start = ((), (), s32[]{:S(2)}) async-start(), calls=%async_computation.1 | async-start | bytes 327680 | tf_op jit(solution)/shard_map/psum | solution.py:48
  358.3 5.0 copy-start.3
  375.7 216.0 %all-reduce.41.cloned.1.call-start = ((), (), s32[]{:S(2)}) async-start(), calls=%async_computation.10 | async-start | bytes 1310720 | tf_op jit(solution)/shard_map/psum | solution.py:9
  512.1 170.4 %all-reduce.25.cloned.1.call-start = ((), (), s32[]{:S(2)}) async-start(), calls=%async_computation.2 | async-start | bytes 327680 | tf_op jit(solution)/shard_map/psum | solution.py:48
  607.8 5.0 copy-start.2
  625.2 215.9 %all-reduce.39.cloned.1.call-start = ((), (), s32[]{:S(2)}) async-start(), calls=%async_computation.9 | async-start | bytes 1310720 | tf_op jit(solution)/shard_map/psum | solution.py:9
  761.6 170.4 %all-reduce.27.cloned.1.call-start = ((), (), s32[]{:S(2)}) async-start(), calls=%async_computation.3 | async-start | bytes 327680 | tf_op jit(solution)/shard_map/psum | solution.py:48
  857.3 5.0 copy-start.1
  874.7 216.0 %all-reduce.37.cloned.1.call-start = ((), (), s32[]{:S(2)}) async-start(), calls=%async_computation.8 | async-start | bytes 1310720 | tf_op jit(solution)/shard_map/psum | solution.py:9
  1011.1 170.4 %all-reduce.29.cloned.1.call-start = ((), (), s32[]{:S(2)}) async-start(), calls=%async_computation.4 | async-start | bytes 327680 | tf_op jit(solution)/shard_map/psum | solution.py:48
  1106.8 5.0 copy-start
  1124.2 215.9 %all-reduce.35.cloned.1.call-start = ((), (), s32[]{:S(2)}) async-start(), calls=%async_computation.7 | async-start | bytes 1310720 | tf_op jit(solution)/shard_map/psum | solution.py:9
  1260.6 170.6 %all-reduce.31.cloned.1.call-start = ((), (), s32[]{:S(2)}) async-start(), calls=%async_computation.5 | async-start | bytes 327680 | tf_op jit(solution)/shard_map/psum | solution.py:48
  1356.5 5.0 copy-start.4
  1373.9 214.3 %all-reduce.33.cloned.1.call-start = ((), (), s32[]{:S(2)}) async-start(), calls=%async_computation.6 | async-start | bytes 655360 | tf_op jit(solution)/shard_map/psum | solution.py:9
  1510.9 92.7 %copy-start.6 = (f32[6,32,160]{2,1,0:T(8,128)}, f32[6,32,160]{2,1,0:T(8,128)S(1)}, u32[]{:S(2)}) copy-start(f32[6,32,160]{2,1,0:T(8,128)S(1)} %constant_dynamic-update-slice_fusion.12) | copy-start | bytes 368644
Sparse Core Ops, SparseCore 0:
  23.3 85.4 all-reduce.44
  126.1 57.1 all-reduce.20
  262.5 79.3 all-reduce.42
  375.8 57.1 all-reduce.22
  512.2 79.4 all-reduce.40
  625.3 57.1 all-reduce.24
  761.7 79.3 all-reduce.38
  874.8 57.1 all-reduce.26
  1011.2 79.4 all-reduce.36
  1124.3 57.1 all-reduce.28
  1260.7 79.3 all-reduce.34
  1374.0 57.1 all-reduce.30
  1510.7 77.3 all-reduce.32
where the time goes:
time: 1620 us; the launch traced here: 1610 us
  waiting for transfers between devices  819 us (51%)
  blocking collectives  528 us (33%)
  matrix products  192 us (12%)
  local copies, waits for them, and re-layouts  52.1 us (3%)
    psum x7, waiting for transfers between devices, broadcast(): return lax.psum(kept, axis)  479 us
    psum x6, blocking collectives, per_device(): gram_block = lax.psum(contract(v_row, x_row, 1, 1), 'pr')  448 us
    psum x6, waiting for transfers between devices, per_device(): x_row = lax.psum(partial_value, 'pc')  340 us
    dot_general x42, matrix products, contract(): lax.dot_general(left_side, right_side, (((left_dim,), (right_dim,)), ((),...  192 us
    all_gather x6, blocking collectives, per_device(): v_row = lax.all_gather(v_panels[panel], 'pc', axis=1, tiled=True)  80.3 us
  transfers between devices with their start and end apart: 13, of which 13 were waited for; matrix products, arithmetic and copies ran while one was open for 1% of the time, Pallas kernels for 0%

commit v1 on v0

--- a/solution.py
+++ b/solution.py
@@ -45,7 +45,7 @@
         v_col = fetch_v_columns(v_row, col_rank, ratio)
         factor = t_panels[panel]
         partial_value = contract(v_col, matrix, 1, 1)
-        x_row = lax.psum(partial_value, "pc")
+        x_row = jnp.sum(lax.all_gather(partial_value, "pc"), axis=0)
         gram_block = lax.psum(contract(v_row, x_row, 1, 1), "pr")
         middle = contract(contract(factor, gram_block, 0, 0), factor, 1, 0)
         w_row = contract(factor, x_row, 0, 0) - 0.5 * contract(middle, v_row, 0, 0)

time: 1620 us -> 1430 us (0.88)
  waiting for transfers between devices: 819 us -> 634 us
    psum x6 -> x0, waiting for transfers between devices: 340 us -> none  [per_device(): x_row = lax.psum(partial_value, 'pc')]
    psum x7, waiting for transfers between devices: 479 us -> 567 us  [broadcast(): return lax.psum(kept, axis)]
    all_gather x0 -> x6, waiting for transfers between devices: none -> 65.8 us  [per_device(): x_row = jnp.sum(lax.all_gather(partial_value, 'pc'), axis=0)]
  transfers between devices with their start and end apart: 13 -> 13, of which waited for: 13 -> 13; matrix products, arithmetic and copies ran while one was open for 1% -> 0% of each run, Pallas kernels for 0% -> 0%
where the time goes in v1:
time: 1430 us
  waiting for transfers between devices  634 us (44%)
  blocking collectives  530 us (37%)
  matrix products  193 us (13%)
  local copies, waits for them, and re-layouts  39.8 us (3%)
  between operations  14.7 us (1%)
    psum x7, waiting for transfers between devices, broadcast(): return lax.psum(kept, axis)  567 us
    psum x6, blocking collectives, per_device(): gram_block = lax.psum(contract(v_row, x_row, 1, 1), 'pr')  448 us
    dot_general x42, matrix products, contract(): lax.dot_general(left_side, right_side, (((left_dim,), (right_dim,)), ((),...  193 us
    all_gather x6, blocking collectives, per_device(): v_row = lax.all_gather(v_panels[panel], 'pc', axis=1, tiled=True)  81.9 us
    all_gather x6, waiting for transfers between devices, per_device(): x_row = jnp.sum(lax.all_gather(partial_value, 'pc'), axis=0)  65.8 us
    unnamed x31, local copies, waits for them, and re-layouts  31.3 us
  transfers between devices with their start and end apart: 13, of which 13 were waited for; matrix products, arithmetic and copies ran while one was open for 0% of the time, Pallas kernels for 0%

profile of v1, /device:TPU:0, one launch (start us, length us, event | category | flops | bytes accessed | tf_op | source)
XLA Modules:
  0.0 1425.4 jit_solution(1500283033392890727)
XLA Ops:
  8.2 13.8 all-gather
  23.2 85.5 %all-reduce.27.cloned.1.call-done = (f32[32,1280]{1,0:T(8,128)}, f32[32,1280]{1,0:T(8,128)}) async-done(((f32[32,1280]{1,0:T(8,128)}, f32[32,1280]{1,0:T(8,128)}), (f32[32,1280]{1,0:T(8,128)}, f32[32,1280]{1,0:T(8,128)})) %all-reduce.27.cloned.1.call-update) | async-done | bytes 327696 | tf_op jit(solution)/shard_map/psum | solution.py:9
  110.6 15.3 %fusion.109 = f32[32,1280]{1,0:T(8,128)} fusion(f32[32,2560]{1,0:T(8,128)S(1)} %constant_dynamic-update-slice_fusion, f32[1280,2560]{1,0:T(8,128)} %param.3), kind=kOutput, calls=%fused_computation.175 | convolution fusion | flops 1258291200 | bytes 13598720 | tf_op jit(solution)/shard_map/dot_general | solution.py:13
  126.1 13.7 all-gather.2
  151.1 74.7 %psum.212 = f32[32,32]{0,1:T(8,128)S(1)} all-reduce(f32[32,32]{0,1:T(8,128)S(1)} %convolution_bitcast_fusion.11), channel_id=1, replica_groups=mesh['pr'=16,'pc'=8] {'pr'}, use_global_device_ids=true, to_apply=%region_3.4 | all-reduce | flops 1024 | bytes 8192 | tf_op jit(solution)/shard_map/psum | solution.py:49
  228.3 80.5 %all-reduce.25.cloned.1.call-done = (f32[32,1280]{1,0:T(8,128)}, f32[32,1280]{1,0:T(8,128)}, f32[32,1280]{1,0:T(8,128)}, f32[32,1280]{1,0:T(8,128)}) async-done(((f32[32,1280]{1,0:T(8,128)}, f32[32,1280]{1,0:T(8,128)}, f32[32,1280]{1,0:T(8,128)}, f32[32,1280]{1,0:T(8,128)}), (f32[32,1280]{1,0:T(8,128)}, f32[32,1280]{1,0:T(8,128)}, f32[32,1280]{1,0:T(8,128)}, ...) | async-done | bytes 655376 | tf_op jit(solution)/shard_map/psum | solution.py:9
  310.7 14.6 %convolution_subtract_fusion.5 = f32[1280,2560]{1,0:T(8,128)S(1)} fusion(f32[1280,2560]{1,0:T(8,128)} %param.3, f32[32,2560]{1,0:T(8,128)S(1)} %constant_dynamic-update-slice_fusion, f32[32,1280]{1,0:T(8,128)} %get-tuple-element.20, f32[32,1280]{1,0:T(8,128)} %get-tuple-element.21, f32[32,1280]{1,0:T(8,128)S(1)} %get-tuple-element.56, ...), kind=kOutput, calls=%fused_computation.5 | convolution fusion | flops 2520268800 | bytes 27197440 | tf_op jit(solution)/shard_map/dot_general | solution.py:13
  330.3 12.4 fusion.110
  342.9 13.6 all-gather.4
  368.3 74.7 %psum.217 = f32[32,32]{0,1:T(8,128)S(1)} all-reduce(f32[32,32]{0,1:T(8,128)S(1)} %convolution_bitcast_fusion.10), channel_id=1, replica_groups=mesh['pr'=16,'pc'=8] {'pr'}, use_global_device_ids=true, to_apply=%region_9.10 | all-reduce | flops 1024 | bytes 8192 | tf_op jit(solution)/shard_map/psum | solution.py:49
  445.0 80.7 %all-reduce.23.cloned.1.call-done = (f32[32,1280]{1,0:T(8,128)}, f32[32,1280]{1,0:T(8,128)}, f32[32,1280]{1,0:T(8,128)}, f32[32,1280]{1,0:T(8,128)}) async-done(((f32[32,1280]{1,0:T(8,128)}, f32[32,1280]{1,0:T(8,128)}, f32[32,1280]{1,0:T(8,128)}, f32[32,1280]{1,0:T(8,128)}), (f32[32,1280]{1,0:T(8,128)}, f32[32,1280]{1,0:T(8,128)}, f32[32,1280]{1,0:T(8,128)}, ...) | async-done | bytes 655376 | tf_op jit(solution)/shard_map/psum | solution.py:9
  527.6 26.4 %convolution_subtract_fusion.4 = f32[1280,2560]{1,0:T(8,128)S(1)} fusion(f32[1280,2560]{1,0:T(8,128)} %copy-done.4, f32[32,2560]{1,0:T(8,128)S(1)} %constant_dynamic-update-slice_fusion.2, f32[32,1280]{1,0:T(8,128)} %get-tuple-element.16, f32[32,1280]{1,0:T(8,128)} %get-tuple-element.17, f32[32,1280]{1,0:T(8,128)S(1)} %get-tuple-element.57, ...), kind=kOutput, calls=%fused_computation.4 | convolution fusion | flops 2520268800 | bytes 27197440 | tf_op jit(solution)/shard_map/dot_general | solution.py:13
  558.9 12.4 fusion.111
  571.5 13.6 all-gather.6
  596.9 74.7 %psum.222 = f32[32,32]{0,1:T(8,128)S(1)} all-reduce(f32[32,32]{0,1:T(8,128)S(1)} %convolution_bitcast_fusion.9), channel_id=1, replica_groups=mesh['pr'=16,'pc'=8] {'pr'}, use_global_device_ids=true, to_apply=%region_15.16 | all-reduce | flops 1024 | bytes 8192 | tf_op jit(solution)/shard_map/psum | solution.py:49
  673.6 80.7 %all-reduce.21.cloned.1.call-done = (f32[32,1280]{1,0:T(8,128)}, f32[32,1280]{1,0:T(8,128)}, f32[32,1280]{1,0:T(8,128)}, f32[32,1280]{1,0:T(8,128)}) async-done(((f32[32,1280]{1,0:T(8,128)}, f32[32,1280]{1,0:T(8,128)}, f32[32,1280]{1,0:T(8,128)}, f32[32,1280]{1,0:T(8,128)}), (f32[32,1280]{1,0:T(8,128)}, f32[32,1280]{1,0:T(8,128)}, f32[32,1280]{1,0:T(8,128)}, ...) | async-done | bytes 655376 | tf_op jit(solution)/shard_map/psum | solution.py:9
  756.2 14.7 %convolution_subtract_fusion.3 = f32[1280,2560]{1,0:T(8,128)S(1)} fusion(f32[1280,2560]{1,0:T(8,128)} %copy-done.2, f32[32,2560]{1,0:T(8,128)S(1)} %constant_dynamic-update-slice_fusion.4, f32[32,1280]{1,0:T(8,128)} %get-tuple-element.12, f32[32,1280]{1,0:T(8,128)} %get-tuple-element.13, f32[32,1280]{1,0:T(8,128)S(1)} %get-tuple-element.58, ...), kind=kOutput, calls=%fused_computation.3 | convolution fusion | flops 2520268800 | bytes 27197440 | tf_op jit(solution)/shard_map/dot_general | solution.py:13
  775.8 12.4 fusion.112
  788.4 13.6 all-gather.8
  813.9 74.7 %psum.227 = f32[32,32]{0,1:T(8,128)S(1)} all-reduce(f32[32,32]{0,1:T(8,128)S(1)} %convolution_bitcast_fusion.8), channel_id=1, replica_groups=mesh['pr'=16,'pc'=8] {'pr'}, use_global_device_ids=true, to_apply=%region_21.22 | all-reduce | flops 1024 | bytes 8192 | tf_op jit(solution)/shard_map/psum | solution.py:49
  890.6 80.7 %all-reduce.19.cloned.1.call-done = (f32[32,1280]{1,0:T(8,128)}, f32[32,1280]{1,0:T(8,128)}, f32[32,1280]{1,0:T(8,128)}, f32[32,1280]{1,0:T(8,128)}) async-done(((f32[32,1280]{1,0:T(8,128)}, f32[32,1280]{1,0:T(8,128)}, f32[32,1280]{1,0:T(8,128)}, f32[32,1280]{1,0:T(8,128)}), (f32[32,1280]{1,0:T(8,128)}, f32[32,1280]{1,0:T(8,128)}, f32[32,1280]{1,0:T(8,128)}, ...) | async-done | bytes 655376 | tf_op jit(solution)/shard_map/psum | solution.py:9
  973.1 14.4 %convolution_subtract_fusion.2 = f32[1280,2560]{1,0:T(8,128)S(1)} fusion(f32[1280,2560]{1,0:T(8,128)} %copy-done.3, f32[32,2560]{1,0:T(8,128)S(1)} %constant_dynamic-update-slice_fusion.6, f32[32,1280]{1,0:T(8,128)} %get-tuple-element.8, f32[32,1280]{1,0:T(8,128)} %get-tuple-element.9, f32[32,1280]{1,0:T(8,128)S(1)} %get-tuple-element.59, ...), kind=kOutput, calls=%fused_computation.2 | convolution fusion | flops 2520268800 | bytes 27197440 | tf_op jit(solution)/shard_map/dot_general | solution.py:13
  992.5 12.4 fusion.113
  1005.1 13.6 all-gather.10
  1030.5 74.7 %psum.232 = f32[32,32]{0,1:T(8,128)S(1)} all-reduce(f32[32,32]{0,1:T(8,128)S(1)} %convolution_bitcast_fusion.7), channel_id=1, replica_groups=mesh['pr'=16,'pc'=8] {'pr'}, use_global_device_ids=true, to_apply=%region_27.28 | all-reduce | flops 1024 | bytes 8192 | tf_op jit(solution)/shard_map/psum | solution.py:49
  1107.2 80.7 %all-reduce.17.cloned.1.call-done = (f32[32,1280]{1,0:T(8,128)}, f32[32,1280]{1,0:T(8,128)}, f32[32,1280]{1,0:T(8,128)}, f32[32,1280]{1,0:T(8,128)}) async-done(((f32[32,1280]{1,0:T(8,128)}, f32[32,1280]{1,0:T(8,128)}, f32[32,1280]{1,0:T(8,128)}, f32[32,1280]{1,0:T(8,128)}), (f32[32,1280]{1,0:T(8,128)}, f32[32,1280]{1,0:T(8,128)}, f32[32,1280]{1,0:T(8,128)}, ...) | async-done | bytes 655376 | tf_op jit(solution)/shard_map/psum | solution.py:9
  1189.8 14.5 %convolution_subtract_fusion.1 = f32[1280,2560]{1,0:T(8,128)S(1)} fusion(f32[1280,2560]{1,0:T(8,128)} %copy-done.1, f32[32,2560]{1,0:T(8,128)S(1)} %constant_dynamic-update-slice_fusion.8, f32[32,1280]{1,0:T(8,128)} %get-tuple-element.4, f32[32,1280]{1,0:T(8,128)} %get-tuple-element.5, f32[32,1280]{1,0:T(8,128)S(1)} %get-tuple-element.60, ...), kind=kOutput, calls=%fused_computation.1 | convolution fusion | flops 2520268800 | bytes 27197440 | tf_op jit(solution)/shard_map/dot_general | solution.py:13
  1209.2 12.4 fusion.114
  1222.0 23.3 %all-gather.29.cloned.1.call-done = f32[256,1280]{1,0:T(8,128)} async-done(((f32[32,1280]{1,0:T(8,128)}), f32[256,1280]{1,0:T(8,128)}) %all-gather.29.cloned.1.call-update) | async-done | bytes 1310736 | tf_op jit(solution)/shard_map/all_gather | solution.py:48
  1247.5 74.8 %psum.237 = f32[32,32]{0,1:T(8,128)S(1)} all-reduce(f32[32,32]{0,1:T(8,128)S(1)} %convolution_bitcast_fusion.6), channel_id=1, replica_groups=mesh['pr'=16,'pc'=8] {'pr'}, use_global_device_ids=true, to_apply=%region_33.34 | all-reduce | flops 1024 | bytes 8192 | tf_op jit(solution)/shard_map/psum | solution.py:49
  1324.5 78.5 %all-reduce.15.cloned.1.call-done = (f32[32,1280]{1,0:T(8,128)}, f32[32,1280]{1,0:T(8,128)}) async-done(((f32[32,1280]{1,0:T(8,128)}, f32[32,1280]{1,0:T(8,128)}), (f32[32,1280]{1,0:T(8,128)}, f32[32,1280]{1,0:T(8,128)})) %all-reduce.15.cloned.1.call-update) | async-done | bytes 327696 | tf_op jit(solution)/shard_map/psum | solution.py:9
  1403.0 15.4 %convolution_subtract_fusion = f32[1280,2560]{1,0:T(8,128)} fusion(f32[1280,2560]{1,0:T(8,128)} %copy-done, f32[32,2560]{1,0:T(8,128)S(1)} %constant_dynamic-update-slice_fusion.10, f32[32,1280]{1,0:T(8,128)} %get-tuple-element.2, f32[32,1280]{1,0:T(8,128)} %get-tuple-element.3, f32[32,1280]{1,0:T(8,128)S(1)} %get-tuple-element.61, f32[32,1280]{1,0:T(8,128)S(1)} %bitcast.180), kind=kOutput, calls=%fused_computation | convolution fusion | flops 2520268800 | bytes 27197440 | tf_op jit(solution)/shard_map/dot_general | solution.py:13
  (118 shorter events, 112.2 us)
Async XLA Ops:
  7.2 218.7 %copy-start.5 = (f32[6,32,32]{2,1,0:T(8,128)S(1)}, f32[6,32,32]{2,1,0:T(8,128)}, u32[]{:S(2)}) copy-start(f32[6,32,32]{2,1,0:T(8,128)} %param.5) | copy-start | bytes 73732
  7.2 101.6 %all-reduce.27.cloned.1.call-start = ((), (), s32[]{:S(2)}) async-start(), calls=%async_computation.12 | async-start | bytes 655360 | tf_op jit(solution)/shard_map/psum | solution.py:9
  23.2 126.1 %all-gather.19.cloned.1.call-start = ((), (), s32[]{:S(2)}) async-start(), calls=%async_computation | async-start | bytes 1474560 | tf_op jit(solution)/shard_map/all_gather | solution.py:48
  126.0 182.9 %all-reduce.25.cloned.1.call-start = ((), (), s32[]{:S(2)}) async-start(), calls=%async_computation.11 | async-start | bytes 1310720 | tf_op jit(solution)/shard_map/psum | solution.py:9
  228.1 138.0 %all-gather.21.cloned.1.call-start = ((), (), s32[]{:S(2)}) async-start(), calls=%async_computation.1 | async-start | bytes 1474560 | tf_op jit(solution)/shard_map/all_gather | solution.py:48
  325.3 5.0 copy-start.4
  342.7 183.0 %all-reduce.23.cloned.1.call-start = ((), (), s32[]{:S(2)}) async-start(), calls=%async_computation.10 | async-start | bytes 1310720 | tf_op jit(solution)/shard_map/psum | solution.py:9
  444.9 149.8 %all-gather.23.cloned.1.call-start = ((), (), s32[]{:S(2)}) async-start(), calls=%async_computation.2 | async-start | bytes 1474560 | tf_op jit(solution)/shard_map/all_gather | solution.py:48
  553.9 5.0 copy-start.2
  571.4 183.0 %all-reduce.21.cloned.1.call-start = ((), (), s32[]{:S(2)}) async-start(), calls=%async_computation.9 | async-start | bytes 1310720 | tf_op jit(solution)/shard_map/psum | solution.py:9
  673.6 138.1 %all-gather.25.cloned.1.call-start = ((), (), s32[]{:S(2)}) async-start(), calls=%async_computation.3 | async-start | bytes 1474560 | tf_op jit(solution)/shard_map/all_gather | solution.py:48
  770.9 5.0 copy-start.3
  788.3 183.0 %all-reduce.19.cloned.1.call-start = ((), (), s32[]{:S(2)}) async-start(), calls=%async_computation.8 | async-start | bytes 1310720 | tf_op jit(solution)/shard_map/psum | solution.py:9
  890.5 137.8 %all-gather.27.cloned.1.call-start = ((), (), s32[]{:S(2)}) async-start(), calls=%async_computation.4 | async-start | bytes 1474560 | tf_op jit(solution)/shard_map/all_gather | solution.py:48
  987.6 5.0 copy-start.1
  1005.0 183.0 %all-reduce.17.cloned.1.call-start = ((), (), s32[]{:S(2)}) async-start(), calls=%async_computation.7 | async-start | bytes 1310720 | tf_op jit(solution)/shard_map/psum | solution.py:9
  1107.2 138.1 %all-gather.29.cloned.1.call-start = ((), (), s32[]{:S(2)}) async-start(), calls=%async_computation.5 | async-start | bytes 1474560 | tf_op jit(solution)/shard_map/all_gather | solution.py:48
  1204.3 5.0 copy-start
  1221.7 181.3 %all-reduce.15.cloned.1.call-start = ((), (), s32[]{:S(2)}) async-start(), calls=%async_computation.6 | async-start | bytes 655360 | tf_op jit(solution)/shard_map/psum | solution.py:9
  1324.5 94.0 %copy-start.6 = (f32[6,32,160]{2,1,0:T(8,128)}, f32[6,32,160]{2,1,0:T(8,128)S(1)}, u32[]{:S(2)}) copy-start(f32[6,32,160]{2,1,0:T(8,128)S(1)} %constant_dynamic-update-slice_fusion.12) | copy-start | bytes 368644
Sparse Core Ops, SparseCore 0:
  23.3 85.4 all-reduce.26
  126.1 23.1 all-gather.18
  228.2 80.6 all-reduce.24
  342.8 23.2 all-gather.20
  445.1 80.5 all-reduce.22
  571.5 23.2 all-gather.22
  673.7 80.5 all-reduce.20
  788.4 23.2 all-gather.24
  890.6 80.5 all-reduce.18
  1005.1 23.1 all-gather.26
  1107.3 80.6 all-reduce.16
  1221.8 23.4 all-gather.28
  1324.4 78.5 all-reduce.14
